TPU v7x, 32 devices: a whole 2x2x4 slice. The times are simulated.
32 devices in a mesh: seq: 4 (over z), head: 8 (over y, x, core).
Axes of the slice: x: 2, y: 2, z: 4, core: 2. Of those that a mesh axis runs over, the one named last changes fastest.
Arguments:
- queries: bfloat16 [4096, 2048], P(('seq', 'head')), may hold values from -6 to 6
- key_rows: bfloat16 [4096, 2048], P(('seq', 'head')), may hold values from -6 to 6
- value_rows: bfloat16 [4096, 2048], P(('seq', 'head')), may hold values from -6 to 6
- ridge_diag: float32 [16, 128], replicated, may hold values from 0.5 to 4
Outputs:
- mixed: bfloat16 [4096, 2048], P(('seq', 'head'))
All inputs are finite; a program needn't handle non-finite values.
Results may differ from a plain program's by a relative error of at most 0.0075.
The roundings to bfloat16 on the way count: a program that leaves them out, or rounds other values in their place, can miss the bound.
Values may be sent and summed in bfloat16 or wider, within the bound.
A program may use at most 64 MiB of HBM per device.

v0:
```python
import functools

import jax
import jax.numpy as jnp
from jax import lax
from jax.experimental import pallas as pl
from jax.experimental.pallas import tpu as pltpu
from jax.sharding import PartitionSpec as P

DK = 128
GROUP = 64
EDGE = 32
PACK = DK // EDGE
STEP_PACKS = 4
EPS = 1e-06
F32 = jnp.float32
BF16 = jnp.bfloat16


def unit(rows):
    wide = rows.astype(F32)
    back = lax.rsqrt(jnp.sum(wide * wide, axis=-1, keepdims=True) + EPS)
    return (wide * back).astype(BF16)


def split3(value):
    high = value.astype(BF16)
    rest = value - high.astype(F32)
    mid = rest.astype(BF16)
    low = (rest - mid.astype(F32)).astype(BF16)
    return high, mid, low


def dot(left, right, contract):
    return lax.dot_general(left, right, ((contract[:1], contract[1:]), ((), ())), preferred_element_type=F32)


def left_stack(parts):
    high, mid, low = parts
    return jnp.concatenate([high, high, mid, high, low, mid], axis=0)


def right_stack(parts):
    high, mid, low = parts
    return jnp.concatenate([high, mid, high, low, high, mid], axis=0)


def sweep_round(rows, lane, sub, turn):
    base = (lane // EDGE) * EDGE
    within = lane - base

    def take(block, pick):
        return jnp.take_along_axis(block, pick, axis=1, mode="promise_in_bounds")

    j = turn
    at, inner = j // 8, j % 8
    first, second = within == j, within == j + 1
    either = jnp.logical_or(first, second)
    pick1, pick2 = base + j, base + j + 1
    row1 = jnp.broadcast_to(rows[at][inner : inner + 1, :], rows[at].shape)
    row2 = jnp.broadcast_to(rows[at][inner + 1 : inner + 2, :], rows[at].shape)
    a, b, d = take(row1, pick1), take(row1, pick2), take(row2, pick2)
    inv1 = 1.0 / a
    ratio = b * inv1
    inv2 = 1.0 / (d - b * ratio)
    scaled1 = jnp.where(first, -1.0, row1) * inv1
    scaled2 = jnp.where(second, -1.0, jnp.where(first, 0.0, row2) - b * scaled1) * inv2
    scaled1 = jnp.where(second, 0.0, scaled1)
    fresh = []
    for v, block in enumerate(rows):
        col1, col2 = take(block, pick1), take(block, pick2)
        gone = either
        if v == at:
            here1, here2 = sub == inner, sub == inner + 1
            col1 = jnp.where(here1, -1.0, col1)
            col2 = jnp.where(here2, -1.0, jnp.where(here1, 0.0, col2) - col1 * ratio)
            col1 = jnp.where(here2, 0.0, col1)
            gone = jnp.logical_or(either, jnp.logical_or(here1, here2))
        else:
            col2 = col2 - col1 * ratio
        fresh.append(jnp.where(gone, 0.0, block) - col1 * scaled1 - col2 * scaled2)
    return fresh


def invert_all(sys_ref, pinv_ref, after_first):
    count = sys_ref.shape[0]
    packs = count // PACK
    lane = lax.broadcasted_iota(jnp.int32, (8, DK), 1)
    sub = lax.broadcasted_iota(jnp.int32, (8, DK), 0)
    lane32 = lax.broadcasted_iota(jnp.int32, (EDGE, DK), 1)
    sub32 = lax.broadcasted_iota(jnp.int32, (EDGE, DK), 0)
    row128 = lax.broadcasted_iota(jnp.int32, (DK, DK), 0) // EDGE
    lane128 = lax.broadcasted_iota(jnp.int32, (DK, DK), 1) // EDGE

    def panel(p, carry):
        @pl.when(p == 1)
        def _():
            after_first()

        start = pl.multiple_of(p * EDGE, EDGE)
        all_rows = []
        for g in range(packs):
            packed = None
            for k in range(PACK):
                piece = sys_ref[g * PACK + k, pl.ds(start, EDGE), :]
                piece = pltpu.roll(piece, lax.rem((k - p) * EDGE + DK, DK), 1)
                packed = piece if packed is None else jnp.where(lane32 // EDGE == k, piece, packed)
            all_rows.append([packed[8 * v : 8 * v + 8, :] for v in range(EDGE // 8)])
        for turn in range(0, EDGE, 2):
            all_rows = [sweep_round(rows, lane, sub, turn) for rows in all_rows]
        for g in range(packs):
            pinv_ref[g] = jnp.concatenate(all_rows[g], axis=0)

        mine = lane32 // EDGE == p
        diag = lane32 - p * EDGE == sub32
        cleared = jnp.logical_or(row128 == p, lane128 == p)

        def update(turn, carry):
            batch = [turn * STEP_PACKS + i for i in range(STEP_PACKS)]
            rows, inverses = [], []
            for g in batch:
                inverses.append(jnp.transpose(left_stack(split3(pinv_ref[g]))))
                for k in range(PACK):
                    rows.append(sys_ref[g * PACK + k, pl.ds(start, EDGE), :])
            rows = [split3(jnp.where(mine, jnp.where(diag, -1.0, 0.0), r)) for r in rows]
            scaled = []
            for i in range(STEP_PACKS):
                for k in range(PACK):
                    left = inverses[i][k * EDGE : (k + 1) * EDGE, :]
                    scaled.append(dot(left, right_stack(rows[i * PACK + k]), (1, 0)))
            change = [dot(left_stack(r), right_stack(split3(t)), (0, 0)) for r, t in zip(rows, scaled)]
            for i, c in enumerate(change):
                s = turn * STEP_PACKS * PACK + i
                sys_ref[s] = jnp.where(cleared, 0.0, sys_ref[s]) + c
            return carry

        return lax.fori_loop(0, packs // STEP_PACKS, update, carry)

    lax.fori_loop(0, PACK, panel, 0)


def whole_kernel(
    owners, shards, q_hbm, k_hbm, v_hbm, ridge_ref, out_hbm,
    q_all, k_all, v_all, sys_ref, vk_ref, pinv_ref, stage, before, gram_total, vk_total, gram_slots, vk_slots,
    send_sems, recv_sems, local_sems, out_send, out_recv, out_local, gram_send, gram_recv, vk_send, vk_recv,
):
    me, shard = lax.axis_index("head"), lax.axis_index("seq")
    rows_each = q_hbm.shape[0]
    width = q_all.shape[1]
    heads = width // DK
    per_source = rows_each // GROUP
    groups = owners * per_source
    moved = ((k_hbm, k_all), (v_hbm, v_all), (q_hbm, q_all))

    def rows_of(source):
        return pl.ds(pl.multiple_of(source * rows_each, rows_each), rows_each)

    def cols_of(owner):
        return pl.ds(pl.multiple_of(owner * width, width), width)

    def incoming(kind, source):
        return pltpu.make_async_remote_copy(
            src_ref=moved[kind][0].at[:, cols_of(source)],
            dst_ref=moved[kind][1].at[rows_of(source), :],
            send_sem=send_sems.at[kind, source],
            recv_sem=recv_sems.at[kind, source],
            device_id={"head": source},
            device_id_type=pl.DeviceIdType.MESH,
        )

    def outgoing(kind, peer):
        return pltpu.make_async_remote_copy(
            src_ref=moved[kind][0].at[:, cols_of(peer)],
            dst_ref=moved[kind][1].at[rows_of(me), :],
            send_sem=send_sems.at[kind, peer],
            recv_sem=recv_sems.at[kind, me],
            device_id={"head": peer},
            device_id_type=pl.DeviceIdType.MESH,
        )

    def own(kind):
        return pltpu.make_async_copy(
            moved[kind][0].at[:, cols_of(me)], moved[kind][1].at[rows_of(me), :], local_sems.at[kind]
        )

    def total_copy(total, slots, send, recv, far, target):
        return pltpu.make_async_remote_copy(
            src_ref=total,
            dst_ref=slots.at[far - 1],
            send_sem=send.at[far - 1],
            recv_sem=recv.at[far - 1],
            device_id={"seq": target},
            device_id_type=pl.DeviceIdType.MESH,
        )

    def send_totals(total, slots, send, recv):
        for far in range(1, shards):
            @pl.when(shard + far < shards)
            def _():
                total_copy(total, slots, send, recv, far, shard + far).start()

    def wait_totals(total, slots, send, recv):
        for far in range(1, shards):
            @pl.when(shard - far >= 0)
            def _():
                total_copy(total, slots, send, recv, far, shard - far).wait_recv()

    def drain_totals(total, slots, send, recv):
        for far in range(1, shards):
            @pl.when(shard + far < shards)
            def _():
                total_copy(total, slots, send, recv, far, shard + far).wait_send()

    barrier = pltpu.get_barrier_semaphore()
    for step in range(1, owners):
        pl.semaphore_signal(barrier, inc=1, device_id={"head": lax.rem(me + step, owners)}, device_id_type=pl.DeviceIdType.MESH)
    for step in range(1, shards):
        pl.semaphore_signal(barrier, inc=1, device_id={"seq": lax.rem(shard + step, shards)}, device_id_type=pl.DeviceIdType.MESH)
    for kind in range(3):
        own(kind).start()
    pl.semaphore_wait(barrier, owners + shards - 2)
    for kind in range(3):
        for step in range(1, owners):
            outgoing(kind, lax.rem(me + step, owners)).start()
    for kind in range(3):
        own(kind).wait()

    eye = lax.broadcasted_iota(jnp.int32, (DK, DK), 0) == lax.broadcasted_iota(jnp.int32, (DK, DK), 1)
    ridges = [jnp.where(eye, ridge_ref[pl.ds(me * heads + h, 1), :], 0.0) for h in range(heads)]

    def rows_in(source, i):
        return pl.ds(pl.multiple_of(source * rows_each + i * GROUP, GROUP), GROUP)

    def keys_in(source, runs):
        @pl.when(source != me)
        def _():
            incoming(0, source).wait_recv()

        adds = []
        for h in range(heads):
            for i in range(per_source):
                ku = unit(k_all[rows_in(source, i), h * DK : (h + 1) * DK])
                k_all[rows_in(source, i), h * DK : (h + 1) * DK] = ku
                adds.append(dot(ku, ku, (0, 0)))
        runs = list(runs)
        for h in range(heads):
            for i in range(per_source):
                sys_ref[h * groups + source * per_source + i] = runs[h] + ridges[h]
                runs[h] = runs[h] + adds[h * per_source + i]
        return tuple(runs)

    zero = tuple(jnp.zeros((DK, DK), F32) for _ in range(heads))
    runs = lax.fori_loop(0, owners, keys_in, zero)
    for h in range(heads):
        gram_total[h] = runs[h]
    send_totals(gram_total, gram_slots, gram_send, gram_recv)

    def values_in(source, runs):
        @pl.when(source != me)
        def _():
            incoming(1, source).wait_recv()

        adds = []
        for h in range(heads):
            for i in range(per_source):
                cols = slice(h * DK, (h + 1) * DK)
                adds.append(dot(k_all[rows_in(source, i), cols], v_all[rows_in(source, i), cols], (0, 0)))
        runs = list(runs)
        for h in range(heads):
            for i in range(per_source):
                vk_ref[h * groups + source * per_source + i] = runs[h]
                runs[h] = runs[h] + adds[h * per_source + i]
        return tuple(runs)

    runs = lax.fori_loop(0, owners, values_in, zero)
    for h in range(heads):
        vk_total[h] = runs[h]

    def sum_slots(slots, total):
        for h in range(heads):
            total[h] = jnp.zeros((DK, DK), F32)
        for far in range(1, shards):
            @pl.when(shard - far >= 0)
            def _():
                for h in range(heads):
                    total[h] = total[h] + slots[far - 1, h]

    wait_totals(gram_total, gram_slots, gram_send, gram_recv)
    sum_slots(gram_slots, before)
    for h in range(heads):
        extra = before[h]

        def add(c, carry):
            sys_ref[h * groups + c] = sys_ref[h * groups + c] + extra
            return carry

        lax.fori_loop(0, groups, add, 0)

    invert_all(sys_ref, pinv_ref, lambda: send_totals(vk_total, vk_slots, vk_send, vk_recv))

    wait_totals(vk_total, vk_slots, vk_send, vk_recv)
    sum_slots(vk_slots, before)
    for step in range(1, owners):
        incoming(2, lax.rem(me + step, owners)).wait_recv()

    def result_copy(peer):
        return pltpu.make_async_remote_copy(
            src_ref=stage.at[peer],
            dst_ref=out_hbm.at[:, cols_of(me)],
            send_sem=out_send.at[peer],
            recv_sem=out_recv.at[me],
            device_id={"head": peer},
            device_id_type=pl.DeviceIdType.MESH,
        )

    sub = lax.broadcasted_iota(jnp.int32, (GROUP, 2 * GROUP), 0)
    lane = lax.broadcasted_iota(jnp.int32, (GROUP, 2 * GROUP), 1)
    twice = lane >= GROUP
    causal = jnp.where(twice, lane - GROUP, lane) <= sub

    def finish(step, carry):
        source = lax.rem(me + 1 + step, owners)
        jobs = [(h, i) for h in range(heads) for i in range(per_source)]
        solved = []
        for h, i in jobs:
            qu = unit(q_all[rows_in(source, i), h * DK : (h + 1) * DK])
            full = jnp.concatenate(split3(sys_ref[h * groups + source * per_source + i]), axis=0)
            solved.append(split3(-dot(jnp.concatenate([qu, qu, qu], axis=1), full, (1, 0))))
        scores, carried = [], []
        for (h, i), (high, mid, low) in zip(jobs, solved):
            ku = k_all[rows_in(source, i), h * DK : (h + 1) * DK]
            ku = jnp.concatenate([ku, ku], axis=0)
            ku = jnp.concatenate([ku, ku, ku], axis=1)
            scores.append(dot(jnp.concatenate([high, mid, low], axis=1), ku, (1, 1)))
            left = jnp.concatenate([high, high, mid, high, low, mid], axis=1)
            start = vk_ref[h * groups + source * per_source + i] + before[h]
            carried.append(dot(left, right_stack(split3(start)), (1, 0)))
        for (h, i), score, carry_in in zip(jobs, scores, carried):
            score = jnp.where(causal, score, 0.0)
            high = score.astype(BF16).astype(F32)
            both = jnp.where(twice, score - high, high).astype(BF16)
            vb = v_all[rows_in(source, i), h * DK : (h + 1) * DK]
            inner = dot(both, jnp.concatenate([vb, vb], axis=0), (1, 0))
            stage[source, i * GROUP : (i + 1) * GROUP, h * DK : (h + 1) * DK] = (carry_in + inner).astype(BF16)

        @pl.when(source != me)
        def _():
            result_copy(source).start()

        return carry

    lax.fori_loop(0, owners, finish, 0)
    mine = pltpu.make_async_copy(stage.at[me], out_hbm.at[:, cols_of(me)], out_local)
    mine.start()
    for step in range(1, owners):
        peer = lax.rem(me + step, owners)
        for kind in range(3):
            outgoing(kind, peer).wait_send()
        result_copy(peer).wait_send()
    for step in range(1, owners):
        source = lax.rem(me + step, owners)
        pltpu.make_async_remote_copy(
            src_ref=stage.at[source],
            dst_ref=out_hbm.at[:, cols_of(source)],
            send_sem=out_send.at[source],
            recv_sem=out_recv.at[source],
            device_id={"head": source},
            device_id_type=pl.DeviceIdType.MESH,
        ).wait_recv()
    mine.wait()
    drain_totals(gram_total, gram_slots, gram_send, gram_recv)
    drain_totals(vk_total, vk_slots, vk_send, vk_recv)


def body(queries, key_rows, value_rows, ridge_diag):
    owners, shards = lax.axis_size("head"), lax.axis_size("seq")
    rows, columns = queries.shape
    width = columns // owners
    heads = width // DK
    tokens = rows * owners
    systems = heads * (tokens // GROUP)
    anywhere = pl.BlockSpec(memory_space=pltpu.HBM)
    dma = pltpu.SemaphoreType.DMA
    return pl.pallas_call(
        functools.partial(whole_kernel, owners, shards),
        out_shape=jax.ShapeDtypeStruct((rows, columns), BF16),
        in_specs=[anywhere] * 3 + [pl.BlockSpec(memory_space=pltpu.VMEM)],
        out_specs=anywhere,
        scratch_shapes=[
            pltpu.VMEM((tokens, width), BF16),
            pltpu.VMEM((tokens, width), BF16),
            pltpu.VMEM((tokens, width), BF16),
            pltpu.VMEM((systems, DK, DK), F32),
            pltpu.VMEM((systems, DK, DK), F32),
            pltpu.VMEM((systems // PACK, EDGE, DK), F32),
            pltpu.VMEM((owners, rows, width), BF16),
            pltpu.VMEM((heads, DK, DK), F32),
            pltpu.VMEM((heads, DK, DK), F32),
            pltpu.VMEM((heads, DK, DK), F32),
            pltpu.VMEM((shards - 1, heads, DK, DK), F32),
            pltpu.VMEM((shards - 1, heads, DK, DK), F32),
            dma((3, owners)), dma((3, owners)), dma((3,)),
            dma((owners,)), dma((owners,)), dma,
            dma((shards - 1,)), dma((shards - 1,)), dma((shards - 1,)), dma((shards - 1,)),
        ],
        compiler_params=pltpu.CompilerParams(
            vmem_limit_bytes=67_000_000, collective_id=0, has_side_effects=True
        ),
    )(queries, key_rows, value_rows, ridge_diag)


def solution(mesh):
    in_specs = (P(("seq", "head"), None), P(("seq", "head"), None), P(("seq", "head"), None), P())
    out_specs = P(("seq", "head"), None)
    return jax.shard_map(body, mesh=mesh, in_specs=in_specs, out_specs=out_specs, check_vma=False)
```

profile of v0, /device:TPU:27, one launch (start us, length us, event | category | flops | bytes accessed | tf_op | source)
XLA Modules:
  0.0 61.0 jit_solution(8983692862300007177)
XLA Ops:
  0.0 59.1 %shard_map.46 = bf16[128,2048]{1,0:T(8,128)(2,1)} custom-call(bf16[128,2048]{1,0:T(8,128)(2,1)} %q_hbm.1, bf16[128,2048]{1,0:T(8,128)(2,1)} %k_hbm.1, bf16[128,2048]{1,0:T(8,128)(2,1)} %v_hbm.1, f32[16,128]{1,0:T(8,128)} %ridge_ref.1), custom_call_target="tpu_custom_call" | custom-call | tf_op jit(solution)/shard_map/pallas_call | solution.py:384
  59.1 1.9 %copy.6 = bf16[128,2048]{1,0:T(8,128)(2,1)} copy(bf16[128,2048]{1,0:T(8,128)(2,1)} %shard_map.46) | data formatting | bytes 1048576
where the time goes:
time: 61.2 us; the launch traced here: 61 us
  Pallas kernels  59.1 us (97%)
  local copies, waits for them, and re-layouts  1.88 us (3%)
    pallas_call x1, Pallas kernels, body(): pl.pallas_call(functools.partial(whole_kernel, owners, shards), out_shape...  59.1 us
    unnamed x1, local copies, waits for them, and re-layouts  1.88 us

commit v1 on v0

--- a/solution.py
+++ b/solution.py
@@ -12,6 +12,7 @@
 EDGE = 32
 PACK = DK // EDGE
 STEP_PACKS = 4
+CHUNK = 64
 EPS = 1e-06
 F32 = jnp.float32
 BF16 = jnp.bfloat16
@@ -82,7 +83,7 @@
     return fresh
 
 
-def invert_all(sys_ref, pinv_ref, after_first):
+def invert_all(sys_ref, pinv_ref, midway):
     count = sys_ref.shape[0]
     packs = count // PACK
     lane = lax.broadcasted_iota(jnp.int32, (8, DK), 1)
@@ -93,9 +94,9 @@
     lane128 = lax.broadcasted_iota(jnp.int32, (DK, DK), 1) // EDGE
 
     def panel(p, carry):
-        @pl.when(p == 1)
+        @pl.when(p == PACK // 2)
         def _():
-            after_first()
+            midway()
 
         start = pl.multiple_of(p * EDGE, EDGE)
         all_rows = []
@@ -141,7 +142,7 @@
 
 def whole_kernel(
     owners, shards, q_hbm, k_hbm, v_hbm, ridge_ref, out_hbm,
-    q_all, k_all, v_all, sys_ref, vk_ref, pinv_ref, stage, before, gram_total, vk_total, gram_slots, vk_slots,
+    q_all, k_all, v_all, sys_ref, vk_ref, pinv_ref, stage, gram_total, vk_total, gram_staged, vk_staged, gram_before, vk_before,
     send_sems, recv_sems, local_sems, out_send, out_recv, out_local, gram_send, gram_recv, vk_send, vk_recv,
 ):
     me, shard = lax.axis_index("head"), lax.axis_index("seq")
@@ -183,55 +184,69 @@
             moved[kind][0].at[:, cols_of(me)], moved[kind][1].at[rows_of(me), :], local_sems.at[kind]
         )
 
-    def total_copy(total, slots, send, recv, far, target):
+    def chunk(c):
+        return c * CHUNK // DK, pl.ds(c * CHUNK % DK, CHUNK)
+
+    def link_copy(staged, before, send, recv, c, target):
+        head, rows = chunk(c)
         return pltpu.make_async_remote_copy(
-            src_ref=total,
-            dst_ref=slots.at[far - 1],
-            send_sem=send.at[far - 1],
-            recv_sem=recv.at[far - 1],
+            src_ref=staged.at[head, rows, :],
+            dst_ref=before.at[head, rows, :],
+            send_sem=send.at[c],
+            recv_sem=recv.at[c],
             device_id={"seq": target},
             device_id_type=pl.DeviceIdType.MESH,
         )
 
-    def send_totals(total, slots, send, recv):
-        for far in range(1, shards):
-            @pl.when(shard + far < shards)
+    chunks = heads * DK // CHUNK
+
+    def chain(total, staged, before, send, recv):
+        for c in range(chunks):
+            head, rows = chunk(c)
+
+            @pl.when(shard > 0)
             def _():
-                total_copy(total, slots, send, recv, far, shard + far).start()
-
-    def wait_totals(total, slots, send, recv):
-        for far in range(1, shards):
-            @pl.when(shard - far >= 0)
+                link_copy(staged, before, send, recv, c, shard).wait_recv()
+
+            @pl.when(shard + 1 < shards)
             def _():
-                total_copy(total, slots, send, recv, far, shard - far).wait_recv()
-
-    def drain_totals(total, slots, send, recv):
-        for far in range(1, shards):
-            @pl.when(shard + far < shards)
+                staged[head, rows, :] = total[head, rows, :] + before[head, rows, :]
+                link_copy(staged, before, send, recv, c, shard + 1).start()
+
+    def drain(staged, before, send, recv):
+        for c in range(chunks):
+            @pl.when(shard + 1 < shards)
             def _():
-                total_copy(total, slots, send, recv, far, shard + far).wait_send()
+                link_copy(staged, before, send, recv, c, shard + 1).wait_send()
 
     barrier = pltpu.get_barrier_semaphore()
     for step in range(1, owners):
         pl.semaphore_signal(barrier, inc=1, device_id={"head": lax.rem(me + step, owners)}, device_id_type=pl.DeviceIdType.MESH)
-    for step in range(1, shards):
-        pl.semaphore_signal(barrier, inc=1, device_id={"seq": lax.rem(shard + step, shards)}, device_id_type=pl.DeviceIdType.MESH)
+    for near in (shard - 1, shard + 1):
+        @pl.when(jnp.logical_and(near >= 0, near < shards))
+        def _():
+            pl.semaphore_signal(barrier, inc=1, device_id={"seq": near}, device_id_type=pl.DeviceIdType.MESH)
     for kind in range(3):
         own(kind).start()
-    pl.semaphore_wait(barrier, owners + shards - 2)
+    ends = (shard == 0).astype(jnp.int32) + (shard == shards - 1).astype(jnp.int32)
+    pl.semaphore_wait(barrier, owners - 1 + 2 - ends)
     for kind in range(3):
         for step in range(1, owners):
             outgoing(kind, lax.rem(me + step, owners)).start()
     for kind in range(3):
         own(kind).wait()
 
-    eye = lax.broadcasted_iota(jnp.int32, (DK, DK), 0) == lax.broadcasted_iota(jnp.int32, (DK, DK), 1)
-    ridges = [jnp.where(eye, ridge_ref[pl.ds(me * heads + h, 1), :], 0.0) for h in range(heads)]
+    @pl.when(shard == 0)
+    def _():
+        gram_before[...] = jnp.zeros_like(gram_before)
+        vk_before[...] = jnp.zeros_like(vk_before)
 
     def rows_in(source, i):
         return pl.ds(pl.multiple_of(source * rows_each + i * GROUP, GROUP), GROUP)
 
-    def keys_in(source, runs):
+    def keys_in(step, runs):
+        source = lax.rem(me + owners - step, owners)
+
         @pl.when(source != me)
         def _():
             incoming(0, source).wait_recv()
@@ -245,7 +260,7 @@
         runs = list(runs)
         for h in range(heads):
             for i in range(per_source):
-                sys_ref[h * groups + source * per_source + i] = runs[h] + ridges[h]
+                sys_ref[h * groups + source * per_source + i] = adds[h * per_source + i]
                 runs[h] = runs[h] + adds[h * per_source + i]
         return tuple(runs)
 
@@ -253,7 +268,7 @@
     runs = lax.fori_loop(0, owners, keys_in, zero)
     for h in range(heads):
         gram_total[h] = runs[h]
-    send_totals(gram_total, gram_slots, gram_send, gram_recv)
+    chain(gram_total, gram_staged, gram_before, gram_send, gram_recv)
 
     def values_in(source, runs):
         @pl.when(source != me)
@@ -272,34 +287,29 @@
                 runs[h] = runs[h] + adds[h * per_source + i]
         return tuple(runs)
 
-    runs = lax.fori_loop(0, owners, values_in, zero)
-    for h in range(heads):
-        vk_total[h] = runs[h]
-
-    def sum_slots(slots, total):
-        for h in range(heads):
-            total[h] = jnp.zeros((DK, DK), F32)
-        for far in range(1, shards):
-            @pl.when(shard - far >= 0)
-            def _():
-                for h in range(heads):
-                    total[h] = total[h] + slots[far - 1, h]
-
-    wait_totals(gram_total, gram_slots, gram_send, gram_recv)
-    sum_slots(gram_slots, before)
-    for h in range(heads):
-        extra = before[h]
-
-        def add(c, carry):
-            sys_ref[h * groups + c] = sys_ref[h * groups + c] + extra
-            return carry
-
-        lax.fori_loop(0, groups, add, 0)
-
-    invert_all(sys_ref, pinv_ref, lambda: send_totals(vk_total, vk_slots, vk_send, vk_recv))
-
-    wait_totals(vk_total, vk_slots, vk_send, vk_recv)
-    sum_slots(vk_slots, before)
+    def values_out():
+        runs = lax.fori_loop(0, owners, values_in, zero)
+        for h in range(heads):
+            vk_total[h] = runs[h]
+        chain(vk_total, vk_staged, vk_before, vk_send, vk_recv)
+
+    eye = lax.broadcasted_iota(jnp.int32, (DK, DK), 0) == lax.broadcasted_iota(jnp.int32, (DK, DK), 1)
+
+    def start_of(c, runs):
+        runs = list(runs)
+        for h in range(heads):
+            own_gram = sys_ref[h * groups + c]
+            sys_ref[h * groups + c] = runs[h]
+            runs[h] = runs[h] + own_gram
+        return tuple(runs)
+
+    lax.fori_loop(
+        0, groups, start_of,
+        tuple(gram_before[h] + jnp.where(eye, ridge_ref[pl.ds(me * heads + h, 1), :], 0.0) for h in range(heads)),
+    )
+
+    invert_all(sys_ref, pinv_ref, values_out)
+
     for step in range(1, owners):
         incoming(2, lax.rem(me + step, owners)).wait_recv()
 
@@ -333,7 +343,7 @@
             ku = jnp.concatenate([ku, ku, ku], axis=1)
             scores.append(dot(jnp.concatenate([high, mid, low], axis=1), ku, (1, 1)))
             left = jnp.concatenate([high, high, mid, high, low, mid], axis=1)
-            start = vk_ref[h * groups + source * per_source + i] + before[h]
+            start = vk_ref[h * groups + source * per_source + i] + vk_before[h]
             carried.append(dot(left, right_stack(split3(start)), (1, 0)))
         for (h, i), score, carry_in in zip(jobs, scores, carried):
             score = jnp.where(causal, score, 0.0)
@@ -368,8 +378,8 @@
             device_id_type=pl.DeviceIdType.MESH,
         ).wait_recv()
     mine.wait()
-    drain_totals(gram_total, gram_slots, gram_send, gram_recv)
-    drain_totals(vk_total, vk_slots, vk_send, vk_recv)
+    drain(gram_staged, gram_before, gram_send, gram_recv)
+    drain(vk_staged, vk_before, vk_send, vk_recv)
 
 
 def body(queries, key_rows, value_rows, ridge_diag):
@@ -394,14 +404,10 @@
             pltpu.VMEM((systems, DK, DK), F32),
             pltpu.VMEM((systems // PACK, EDGE, DK), F32),
             pltpu.VMEM((owners, rows, width), BF16),
-            pltpu.VMEM((heads, DK, DK), F32),
-            pltpu.VMEM((heads, DK, DK), F32),
-            pltpu.VMEM((heads, DK, DK), F32),
-            pltpu.VMEM((shards - 1, heads, DK, DK), F32),
-            pltpu.VMEM((shards - 1, heads, DK, DK), F32),
+            *[pltpu.VMEM((heads, DK, DK), F32)] * 6,
             dma((3, owners)), dma((3, owners)), dma((3,)),
             dma((owners,)), dma((owners,)), dma,
-            dma((shards - 1,)), dma((shards - 1,)), dma((shards - 1,)), dma((shards - 1,)),
+            *[dma((heads * DK // CHUNK,))] * 4,
         ],
         compiler_params=pltpu.CompilerParams(
             vmem_limit_bytes=67_000_000, collective_id=0, has_side_effects=True

time: 61.2 us -> 52.9 us (0.86)
  Pallas kernels: 59.1 us -> 50.9 us
    pallas_call x1, Pallas kernels: 59.1 us -> 50.9 us  [body(): pl.pallas_call(functools.partial(whole_kernel, owners, shards), out_shape...]
where the time goes in v1:
time: 52.9 us; the launch traced here: 52.7 us
  Pallas kernels  50.9 us (96%)
  local copies, waits for them, and re-layouts  1.88 us (4%)
    pallas_call x1, Pallas kernels, body(): pl.pallas_call(functools.partial(whole_kernel, owners, shards), out_shape...  50.9 us
    unnamed x1, local copies, waits for them, and re-layouts  1.88 us

profile of v1, /device:TPU:27, one launch (start us, length us, event | category | flops | bytes accessed | tf_op | source)
XLA Modules:
  0.0 52.7 jit_solution(12103255739536699310)
XLA Ops:
  0.0 50.9 %shard_map.46 = bf16[128,2048]{1,0:T(8,128)(2,1)} custom-call(bf16[128,2048]{1,0:T(8,128)(2,1)} %q_hbm.1, bf16[128,2048]{1,0:T(8,128)(2,1)} %k_hbm.1, bf16[128,2048]{1,0:T(8,128)(2,1)} %v_hbm.1, f32[16,128]{1,0:T(8,128)} %ridge_ref.1), custom_call_target="tpu_custom_call" | custom-call | tf_op jit(solution)/shard_map/pallas_call | solution.py:394
  50.9 1.9 %copy.6 = bf16[128,2048]{1,0:T(8,128)(2,1)} copy(bf16[128,2048]{1,0:T(8,128)(2,1)} %shard_map.46) | data formatting | bytes 1048576

commit v2 on v1

--- a/solution.py
+++ b/solution.py
@@ -10,8 +10,8 @@
 DK = 128
 GROUP = 64
 EDGE = 32
-PACK = DK // EDGE
-STEP_PACKS = 4
+BATCH = 16
+SUBLANES = 8
 CHUNK = 64
 EPS = 1e-06
 F32 = jnp.float32
@@ -46,103 +46,117 @@
     return jnp.concatenate([high, mid, high, low, high, mid], axis=0)
 
 
-def sweep_round(rows, lane, sub, turn):
-    base = (lane // EDGE) * EDGE
-    within = lane - base
+def sweep_pair(tiles, turn, lane, sub):
+    at, inner = turn // SUBLANES, turn % SUBLANES
+    within = lane % SUBLANES
+    pick1 = lane - within + inner
+    pick2 = pick1 + 1
+    first, second = within == inner, within == inner + 1
+    either = jnp.logical_or(first, second)
+    here1, here2 = sub == inner, sub == inner + 1
+    here = jnp.logical_or(here1, here2)
 
     def take(block, pick):
         return jnp.take_along_axis(block, pick, axis=1, mode="promise_in_bounds")
 
-    j = turn
-    at, inner = j // 8, j % 8
-    first, second = within == j, within == j + 1
-    either = jnp.logical_or(first, second)
-    pick1, pick2 = base + j, base + j + 1
-    row1 = jnp.broadcast_to(rows[at][inner : inner + 1, :], rows[at].shape)
-    row2 = jnp.broadcast_to(rows[at][inner + 1 : inner + 2, :], rows[at].shape)
-    a, b, d = take(row1, pick1), take(row1, pick2), take(row2, pick2)
-    inv1 = 1.0 / a
-    ratio = b * inv1
-    inv2 = 1.0 / (d - b * ratio)
-    scaled1 = jnp.where(first, -1.0, row1) * inv1
-    scaled2 = jnp.where(second, -1.0, jnp.where(first, 0.0, row2) - b * scaled1) * inv2
-    scaled1 = jnp.where(second, 0.0, scaled1)
+    def spread(block, row):
+        return jnp.broadcast_to(block[row : row + 1, :], block.shape)
+
+    col1 = [take(block, pick1) for block in tiles[at]]
+    col2 = [take(block, pick2) for block in tiles[at]]
+    a, b, d = spread(col1[at], inner), spread(col2[at], inner), spread(col2[at], inner + 1)
+    back = 1.0 / (a * d - b * b)
+    e, f, h = d * back, b * back, a * back
+    col1[at] = jnp.where(here1, -1.0, jnp.where(here2, 0.0, col1[at]))
+    col2[at] = jnp.where(here2, -1.0, jnp.where(here1, 0.0, col2[at]))
     fresh = []
-    for v, block in enumerate(rows):
-        col1, col2 = take(block, pick1), take(block, pick2)
-        gone = either
-        if v == at:
-            here1, here2 = sub == inner, sub == inner + 1
-            col1 = jnp.where(here1, -1.0, col1)
-            col2 = jnp.where(here2, -1.0, jnp.where(here1, 0.0, col2) - col1 * ratio)
-            col1 = jnp.where(here2, 0.0, col1)
-            gone = jnp.logical_or(either, jnp.logical_or(here1, here2))
-        else:
-            col2 = col2 - col1 * ratio
-        fresh.append(jnp.where(gone, 0.0, block) - col1 * scaled1 - col2 * scaled2)
+    for g, column in enumerate(tiles):
+        row1, row2 = spread(column[at], inner), spread(column[at], inner + 1)
+        if g == at:
+            row1 = jnp.where(first, -1.0, jnp.where(second, 0.0, row1))
+            row2 = jnp.where(second, -1.0, jnp.where(first, 0.0, row2))
+        scaled1, scaled2 = e * row1 - f * row2, h * row2 - f * row1
+        blocks = []
+        for v, block in enumerate(column):
+            if v == at:
+                block = jnp.where(here, 0.0, block)
+            if g == at:
+                block = jnp.where(either, 0.0, block)
+            blocks.append(block - (col1[v] * scaled1 + col2[v] * scaled2))
+        fresh.append(blocks)
     return fresh
 
 
-def invert_all(sys_ref, pinv_ref, midway):
-    count = sys_ref.shape[0]
-    packs = count // PACK
-    lane = lax.broadcasted_iota(jnp.int32, (8, DK), 1)
-    sub = lax.broadcasted_iota(jnp.int32, (8, DK), 0)
+def invert_all(count, sys_ref, turn_ref, pinv_ref, midway):
+    copies = DK // EDGE
+    share = DK // SUBLANES
+    bands = EDGE // SUBLANES
+    lane = lax.broadcasted_iota(jnp.int32, (SUBLANES, DK), 1)
+    sub = lax.broadcasted_iota(jnp.int32, (SUBLANES, DK), 0)
     lane32 = lax.broadcasted_iota(jnp.int32, (EDGE, DK), 1)
     sub32 = lax.broadcasted_iota(jnp.int32, (EDGE, DK), 0)
     row128 = lax.broadcasted_iota(jnp.int32, (DK, DK), 0) // EDGE
     lane128 = lax.broadcasted_iota(jnp.int32, (DK, DK), 1) // EDGE
 
     def panel(p, carry):
-        @pl.when(p == PACK // 2)
+        @pl.when(p == copies // 2)
         def _():
             midway()
 
         start = pl.multiple_of(p * EDGE, EDGE)
-        all_rows = []
-        for g in range(packs):
-            packed = None
-            for k in range(PACK):
-                piece = sys_ref[g * PACK + k, pl.ds(start, EDGE), :]
-                piece = pltpu.roll(piece, lax.rem((k - p) * EDGE + DK, DK), 1)
-                packed = piece if packed is None else jnp.where(lane32 // EDGE == k, piece, packed)
-            all_rows.append([packed[8 * v : 8 * v + 8, :] for v in range(EDGE // 8)])
+        halves = []
+        for half in range(count // share):
+            tiles = []
+            for g in range(bands):
+                at = half * bands + g
+                stacked = [
+                    sys_ref[pl.ds(pl.multiple_of((half * share + s) * DK + start + g * SUBLANES, SUBLANES), SUBLANES), :]
+                    for s in range(share)
+                ]
+                turn_ref[at] = jnp.transpose(jnp.concatenate(stacked, axis=0))
+                tiles.append([
+                    turn_ref[at, pl.ds(pl.multiple_of(start + v * SUBLANES, SUBLANES), SUBLANES), :] for v in range(bands)
+                ])
+            halves.append(tiles)
         for turn in range(0, EDGE, 2):
-            all_rows = [sweep_round(rows, lane, sub, turn) for rows in all_rows]
-        for g in range(packs):
-            pinv_ref[g] = jnp.concatenate(all_rows[g], axis=0)
+            halves = [sweep_pair(tiles, turn, lane, sub) for tiles in halves]
+        for half, tiles in enumerate(halves):
+            for g, column in enumerate(tiles):
+                block = jnp.transpose(jnp.concatenate(column * copies, axis=0))
+                for s in range(share):
+                    row = (half * share + s) * EDGE + g * SUBLANES
+                    pinv_ref[row : row + SUBLANES, :] = block[s * SUBLANES : (s + 1) * SUBLANES, :]
 
         mine = lane32 // EDGE == p
         diag = lane32 - p * EDGE == sub32
         cleared = jnp.logical_or(row128 == p, lane128 == p)
+        third = lane32 // EDGE == 2
+        first = lane32 // EDGE == 0
 
         def update(turn, carry):
-            batch = [turn * STEP_PACKS + i for i in range(STEP_PACKS)]
-            rows, inverses = [], []
+            batch = [turn * BATCH + i for i in range(BATCH)]
+            lefts, rows = [], []
             for g in batch:
-                inverses.append(jnp.transpose(left_stack(split3(pinv_ref[g]))))
-                for k in range(PACK):
-                    rows.append(sys_ref[g * PACK + k, pl.ds(start, EDGE), :])
-            rows = [split3(jnp.where(mine, jnp.where(diag, -1.0, 0.0), r)) for r in rows]
-            scaled = []
-            for i in range(STEP_PACKS):
-                for k in range(PACK):
-                    left = inverses[i][k * EDGE : (k + 1) * EDGE, :]
-                    scaled.append(dot(left, right_stack(rows[i * PACK + k]), (1, 0)))
+                high, mid, low = split3(pinv_ref[pl.ds(pl.multiple_of(g * EDGE, EDGE), EDGE), :])
+                left = jnp.concatenate([jnp.where(third, mid, high), jnp.where(first, low, mid)], axis=1)
+                lefts.append(left[:, : 6 * EDGE])
+                row = sys_ref[pl.ds(pl.multiple_of(g * DK, DK) + start, EDGE), :]
+                rows.append(split3(jnp.where(mine, jnp.where(diag, -1.0, 0.0), row)))
+            scaled = [dot(left, right_stack(r), (1, 0)) for left, r in zip(lefts, rows)]
             change = [dot(left_stack(r), right_stack(split3(t)), (0, 0)) for r, t in zip(rows, scaled)]
-            for i, c in enumerate(change):
-                s = turn * STEP_PACKS * PACK + i
-                sys_ref[s] = jnp.where(cleared, 0.0, sys_ref[s]) + c
+            for g, c in zip(batch, change):
+                whole = pl.ds(pl.multiple_of(g * DK, DK), DK)
+                sys_ref[whole, :] = jnp.where(cleared, 0.0, sys_ref[whole, :]) + c
             return carry
 
-        return lax.fori_loop(0, packs // STEP_PACKS, update, carry)
-
-    lax.fori_loop(0, PACK, panel, 0)
+        return lax.fori_loop(0, count // BATCH, update, carry)
+
+    lax.fori_loop(0, copies, panel, 0)
 
 
 def whole_kernel(
     owners, shards, q_hbm, k_hbm, v_hbm, ridge_ref, out_hbm,
-    q_all, k_all, v_all, sys_ref, vk_ref, pinv_ref, stage, gram_total, vk_total, gram_staged, vk_staged, gram_before, vk_before,
+    q_all, k_all, v_all, sys_ref, vk_ref, turn_ref, pinv_ref, stage, gram_total, vk_total, gram_staged, vk_staged, gram_before, vk_before,
     send_sems, recv_sems, local_sems, out_send, out_recv, out_local, gram_send, gram_recv, vk_send, vk_recv,
 ):
     me, shard = lax.axis_index("head"), lax.axis_index("seq")
@@ -241,6 +255,9 @@
         gram_before[...] = jnp.zeros_like(gram_before)
         vk_before[...] = jnp.zeros_like(vk_before)
 
+    def system(head, group):
+        return pl.ds(pl.multiple_of((head * groups + group) * DK, DK), DK)
+
     def rows_in(source, i):
         return pl.ds(pl.multiple_of(source * rows_each + i * GROUP, GROUP), GROUP)
 
@@ -260,7 +277,7 @@
         runs = list(runs)
         for h in range(heads):
             for i in range(per_source):
-                sys_ref[h * groups + source * per_source + i] = adds[h * per_source + i]
+                sys_ref[system(h, source * per_source + i), :] = adds[h * per_source + i]
                 runs[h] = runs[h] + adds[h * per_source + i]
         return tuple(runs)
 
@@ -298,8 +315,8 @@
     def start_of(c, runs):
         runs = list(runs)
         for h in range(heads):
-            own_gram = sys_ref[h * groups + c]
-            sys_ref[h * groups + c] = runs[h]
+            own_gram = sys_ref[system(h, c), :]
+            sys_ref[system(h, c), :] = runs[h]
             runs[h] = runs[h] + own_gram
         return tuple(runs)
 
@@ -308,7 +325,7 @@
         tuple(gram_before[h] + jnp.where(eye, ridge_ref[pl.ds(me * heads + h, 1), :], 0.0) for h in range(heads)),
     )
 
-    invert_all(sys_ref, pinv_ref, values_out)
+    invert_all(heads * groups, sys_ref, turn_ref, pinv_ref, values_out)
 
     for step in range(1, owners):
         incoming(2, lax.rem(me + step, owners)).wait_recv()
@@ -334,7 +351,7 @@
         solved = []
         for h, i in jobs:
             qu = unit(q_all[rows_in(source, i), h * DK : (h + 1) * DK])
-            full = jnp.concatenate(split3(sys_ref[h * groups + source * per_source + i]), axis=0)
+            full = jnp.concatenate(split3(sys_ref[system(h, source * per_source + i), :]), axis=0)
             solved.append(split3(-dot(jnp.concatenate([qu, qu, qu], axis=1), full, (1, 0))))
         scores, carried = [], []
         for (h, i), (high, mid, low) in zip(jobs, solved):
@@ -400,9 +417,10 @@
             pltpu.VMEM((tokens, width), BF16),
             pltpu.VMEM((tokens, width), BF16),
             pltpu.VMEM((tokens, width), BF16),
+            pltpu.VMEM((systems * DK, DK), F32),
             pltpu.VMEM((systems, DK, DK), F32),
-            pltpu.VMEM((systems, DK, DK), F32),
-            pltpu.VMEM((systems // PACK, EDGE, DK), F32),
+            pltpu.VMEM((systems * EDGE // DK, DK, DK), F32),
+            pltpu.VMEM((systems * EDGE, DK), F32),
             pltpu.VMEM((owners, rows, width), BF16),
             *[pltpu.VMEM((heads, DK, DK), F32)] * 6,
             dma((3, owners)), dma((3, owners)), dma((3,)),

time: 52.9 us -> 51 us (0.964)
  Pallas kernels: 50.9 us -> 48.9 us
    pallas_call x1, Pallas kernels: 50.9 us -> 48.9 us  [body(): pl.pallas_call(functools.partial(whole_kernel, owners, shards), out_shape...]
where the time goes in v2:
time: 51 us; the launch traced here: 50.8 us
  Pallas kernels  48.9 us (96%)
  local copies, waits for them, and re-layouts  1.88 us (4%)
    pallas_call x1, Pallas kernels, body(): pl.pallas_call(functools.partial(whole_kernel, owners, shards), out_shape...  48.9 us
    unnamed x1, local copies, waits for them, and re-layouts  1.88 us

profile of v2, /device:TPU:27, one launch (start us, length us, event | category | flops | bytes accessed | tf_op | source)
XLA Modules:
  0.0 50.8 jit_solution(5235005307328219142)
XLA Ops:
  0.0 48.9 %shard_map.46 = bf16[128,2048]{1,0:T(8,128)(2,1)} custom-call(bf16[128,2048]{1,0:T(8,128)(2,1)} %q_hbm.1, bf16[128,2048]{1,0:T(8,128)(2,1)} %k_hbm.1, bf16[128,2048]{1,0:T(8,128)(2,1)} %v_hbm.1, f32[16,128]{1,0:T(8,128)} %ridge_ref.1), custom_call_target="tpu_custom_call" | custom-call | tf_op jit(solution)/shard_map/pallas_call | solution.py:411
  48.9 1.9 %copy.6 = bf16[128,2048]{1,0:T(8,128)(2,1)} copy(bf16[128,2048]{1,0:T(8,128)(2,1)} %shard_map.46) | data formatting | bytes 1048576

commit v3 on v2

--- a/solution.py
+++ b/solution.py
@@ -165,7 +165,21 @@
     heads = width // DK
     per_source = rows_each // GROUP
     groups = owners * per_source
-    moved = ((k_hbm, k_all), (v_hbm, v_all), (q_hbm, q_all))
+    moved = [(k_hbm, k_all, h * DK, DK) for h in range(heads)]
+    moved += [(v_hbm, v_all, 0, width), (q_hbm, q_all, 0, width)]
+    values, queries = heads, heads + 1
+    middle = sorted(range(2, owners - 1), key=lambda step: abs(step - owners // 2))
+    odd = lax.rem(me, 2)
+    partner = owners - 1 - odd * (owners - 2)
+
+    def pick(order, at):
+        step = order[-1]
+        for i, choice in enumerate(order[:-1]):
+            step = jnp.where(at == i, choice, step)
+        return step
+
+    order_out = [*middle, partner, owners - partner]
+    order_in = [0, owners - partner, *middle, partner]
 
     def rows_of(source):
         return pl.ds(pl.multiple_of(source * rows_each, rows_each), rows_each)
@@ -173,10 +187,18 @@
     def cols_of(owner):
         return pl.ds(pl.multiple_of(owner * width, width), width)
 
+    def source_part(kind, owner):
+        ref, _, offset, size = moved[kind]
+        return ref.at[:, pl.ds(pl.multiple_of(owner * width + offset, size), size)]
+
+    def target_part(kind, source):
+        _, ref, offset, size = moved[kind]
+        return ref.at[rows_of(source), pl.ds(offset, size)]
+
     def incoming(kind, source):
         return pltpu.make_async_remote_copy(
-            src_ref=moved[kind][0].at[:, cols_of(source)],
-            dst_ref=moved[kind][1].at[rows_of(source), :],
+            src_ref=source_part(kind, source),
+            dst_ref=target_part(kind, source),
             send_sem=send_sems.at[kind, source],
             recv_sem=recv_sems.at[kind, source],
             device_id={"head": source},
@@ -185,8 +207,8 @@
 
     def outgoing(kind, peer):
         return pltpu.make_async_remote_copy(
-            src_ref=moved[kind][0].at[:, cols_of(peer)],
-            dst_ref=moved[kind][1].at[rows_of(me), :],
+            src_ref=source_part(kind, peer),
+            dst_ref=target_part(kind, me),
             send_sem=send_sems.at[kind, peer],
             recv_sem=recv_sems.at[kind, me],
             device_id={"head": peer},
@@ -194,9 +216,7 @@
         )
 
     def own(kind):
-        return pltpu.make_async_copy(
-            moved[kind][0].at[:, cols_of(me)], moved[kind][1].at[rows_of(me), :], local_sems.at[kind]
-        )
+        return pltpu.make_async_copy(source_part(kind, me), target_part(kind, me), local_sems.at[kind])
 
     def chunk(c):
         return c * CHUNK // DK, pl.ds(c * CHUNK % DK, CHUNK)
@@ -214,13 +234,17 @@
 
     chunks = heads * DK // CHUNK
 
+    def pass_on(total, staged, before, send, recv, only=None):
+        for c in range(chunks):
+            head, rows = chunk(c)
+            if only in (None, head):
+                staged[head, rows, :] = total[head, rows, :] + before[head, rows, :]
+                link_copy(staged, before, send, recv, c, shard + 1).start()
+
     def chain(total, staged, before, send, recv):
         for c in range(chunks):
             head, rows = chunk(c)
-
-            @pl.when(shard > 0)
-            def _():
-                link_copy(staged, before, send, recv, c, shard).wait_recv()
+            link_copy(staged, before, send, recv, c, shard).wait_recv()
 
             @pl.when(shard + 1 < shards)
             def _():
@@ -240,14 +264,14 @@
         @pl.when(jnp.logical_and(near >= 0, near < shards))
         def _():
             pl.semaphore_signal(barrier, inc=1, device_id={"seq": near}, device_id_type=pl.DeviceIdType.MESH)
-    for kind in range(3):
+    for kind in range(len(moved)):
         own(kind).start()
     ends = (shard == 0).astype(jnp.int32) + (shard == shards - 1).astype(jnp.int32)
     pl.semaphore_wait(barrier, owners - 1 + 2 - ends)
-    for kind in range(3):
-        for step in range(1, owners):
+    for kind in range(len(moved)):
+        for step in order_out:
             outgoing(kind, lax.rem(me + step, owners)).start()
-    for kind in range(3):
+    for kind in range(len(moved)):
         own(kind).wait()
 
     @pl.when(shard == 0)
@@ -261,36 +285,45 @@
     def rows_in(source, i):
         return pl.ds(pl.multiple_of(source * rows_each + i * GROUP, GROUP), GROUP)
 
-    def keys_in(step, runs):
-        source = lax.rem(me + owners - step, owners)
-
-        @pl.when(source != me)
-        def _():
-            incoming(0, source).wait_recv()
-
-        adds = []
-        for h in range(heads):
+    def keys_of(h):
+        cols = slice(h * DK, (h + 1) * DK)
+
+        def keys_in(at, run):
+            source = lax.rem(me + owners - pick(order_in, at), owners)
+
+            @pl.when(source != me)
+            def _():
+                incoming(h, source).wait_recv()
+
+            adds = []
             for i in range(per_source):
-                ku = unit(k_all[rows_in(source, i), h * DK : (h + 1) * DK])
-                k_all[rows_in(source, i), h * DK : (h + 1) * DK] = ku
+                ku = unit(k_all[rows_in(source, i), cols])
+                k_all[rows_in(source, i), cols] = ku
                 adds.append(dot(ku, ku, (0, 0)))
-        runs = list(runs)
-        for h in range(heads):
             for i in range(per_source):
-                sys_ref[system(h, source * per_source + i), :] = adds[h * per_source + i]
-                runs[h] = runs[h] + adds[h * per_source + i]
-        return tuple(runs)
+                sys_ref[system(h, source * per_source + i), :] = adds[i]
+                run = run + adds[i]
+            return run
+
+        gram_total[h] = lax.fori_loop(0, owners, keys_in, jnp.zeros((DK, DK), F32))
 
     zero = tuple(jnp.zeros((DK, DK), F32) for _ in range(heads))
-    runs = lax.fori_loop(0, owners, keys_in, zero)
     for h in range(heads):
-        gram_total[h] = runs[h]
-    chain(gram_total, gram_staged, gram_before, gram_send, gram_recv)
+        keys_of(h)
+
+        @pl.when(shard == 0)
+        def _():
+            pass_on(gram_total, gram_staged, gram_before, gram_send, gram_recv, h)
+
+    @pl.when(shard > 0)
+    def _():
+        chain(gram_total, gram_staged, gram_before, gram_send, gram_recv)
+
 
     def values_in(source, runs):
         @pl.when(source != me)
         def _():
-            incoming(1, source).wait_recv()
+            incoming(values, source).wait_recv()
 
         adds = []
         for h in range(heads):
@@ -308,7 +341,14 @@
         runs = lax.fori_loop(0, owners, values_in, zero)
         for h in range(heads):
             vk_total[h] = runs[h]
-        chain(vk_total, vk_staged, vk_before, vk_send, vk_recv)
+
+        @pl.when(shard == 0)
+        def _():
+            pass_on(vk_total, vk_staged, vk_before, vk_send, vk_recv)
+
+        @pl.when(shard > 0)
+        def _():
+            chain(vk_total, vk_staged, vk_before, vk_send, vk_recv)
 
     eye = lax.broadcasted_iota(jnp.int32, (DK, DK), 0) == lax.broadcasted_iota(jnp.int32, (DK, DK), 1)
 
@@ -328,7 +368,7 @@
     invert_all(heads * groups, sys_ref, turn_ref, pinv_ref, values_out)
 
     for step in range(1, owners):
-        incoming(2, lax.rem(me + step, owners)).wait_recv()
+        incoming(queries, lax.rem(me + step, owners)).wait_recv()
 
     def result_copy(peer):
         return pltpu.make_async_remote_copy(
@@ -346,7 +386,7 @@
     causal = jnp.where(twice, lane - GROUP, lane) <= sub
 
     def finish(step, carry):
-        source = lax.rem(me + 1 + step, owners)
+        source = lax.rem(me + pick([*order_out, 0], step), owners)
         jobs = [(h, i) for h in range(heads) for i in range(per_source)]
         solved = []
         for h, i in jobs:
@@ -381,7 +421,7 @@
     mine.start()
     for step in range(1, owners):
         peer = lax.rem(me + step, owners)
-        for kind in range(3):
+        for kind in range(len(moved)):
             outgoing(kind, peer).wait_send()
         result_copy(peer).wait_send()
     for step in range(1, owners):
@@ -423,7 +463,7 @@
             pltpu.VMEM((systems * EDGE, DK), F32),
             pltpu.VMEM((owners, rows, width), BF16),
             *[pltpu.VMEM((heads, DK, DK), F32)] * 6,
-            dma((3, owners)), dma((3, owners)), dma((3,)),
+            dma((heads + 2, owners)), dma((heads + 2, owners)), dma((heads + 2,)),
             dma((owners,)), dma((owners,)), dma,
             *[dma((heads * DK // CHUNK,))] * 4,
         ],

time: 51 us -> 51.7 us (1.014)
  Pallas kernels: 48.9 us -> 49.6 us
    pallas_call x1, Pallas kernels: 48.9 us -> 49.6 us  [body(): pl.pallas_call(functools.partial(whole_kernel, owners, shards), out_shape...]
where the time goes in v3:
time: 51.7 us; the launch traced here: 51.5 us
  Pallas kernels  49.6 us (96%)
  local copies, waits for them, and re-layouts  1.88 us (4%)
    pallas_call x1, Pallas kernels, body(): pl.pallas_call(functools.partial(whole_kernel, owners, shards), out_shape...  49.6 us
    unnamed x1, local copies, waits for them, and re-layouts  1.88 us

profile of v3, /device:TPU:27, one launch (start us, length us, event | category | flops | bytes accessed | tf_op | source)
XLA Modules:
  0.0 51.5 jit_solution(5375159924668356498)
XLA Ops:
  0.0 49.6 %shard_map.46 = bf16[128,2048]{1,0:T(8,128)(2,1)} custom-call(bf16[128,2048]{1,0:T(8,128)(2,1)} %q_hbm.1, bf16[128,2048]{1,0:T(8,128)(2,1)} %k_hbm.1, bf16[128,2048]{1,0:T(8,128)(2,1)} %v_hbm.1, f32[16,128]{1,0:T(8,128)} %ridge_ref.1), custom_call_target="tpu_custom_call" | custom-call | tf_op jit(solution)/shard_map/pallas_call | solution.py:451
  49.6 1.9 %copy.6 = bf16[128,2048]{1,0:T(8,128)(2,1)} copy(bf16[128,2048]{1,0:T(8,128)(2,1)} %shard_map.46) | data formatting | bytes 1048576

commit v4 on v3

--- a/solution.py
+++ b/solution.py
@@ -168,18 +168,6 @@
     moved = [(k_hbm, k_all, h * DK, DK) for h in range(heads)]
     moved += [(v_hbm, v_all, 0, width), (q_hbm, q_all, 0, width)]
     values, queries = heads, heads + 1
-    middle = sorted(range(2, owners - 1), key=lambda step: abs(step - owners // 2))
-    odd = lax.rem(me, 2)
-    partner = owners - 1 - odd * (owners - 2)
-
-    def pick(order, at):
-        step = order[-1]
-        for i, choice in enumerate(order[:-1]):
-            step = jnp.where(at == i, choice, step)
-        return step
-
-    order_out = [*middle, partner, owners - partner]
-    order_in = [0, owners - partner, *middle, partner]
 
     def rows_of(source):
         return pl.ds(pl.multiple_of(source * rows_each, rows_each), rows_each)
@@ -269,7 +257,7 @@
     ends = (shard == 0).astype(jnp.int32) + (shard == shards - 1).astype(jnp.int32)
     pl.semaphore_wait(barrier, owners - 1 + 2 - ends)
     for kind in range(len(moved)):
-        for step in order_out:
+        for step in range(1, owners):
             outgoing(kind, lax.rem(me + step, owners)).start()
     for kind in range(len(moved)):
         own(kind).wait()
@@ -289,7 +277,7 @@
         cols = slice(h * DK, (h + 1) * DK)
 
         def keys_in(at, run):
-            source = lax.rem(me + owners - pick(order_in, at), owners)
+            source = lax.rem(me + owners - at, owners)
 
             @pl.when(source != me)
             def _():
@@ -311,7 +299,7 @@
     for h in range(heads):
         keys_of(h)
 
-        @pl.when(shard == 0)
+        @pl.when(jnp.logical_and(shard == 0, shard + 1 < shards))
         def _():
             pass_on(gram_total, gram_staged, gram_before, gram_send, gram_recv, h)
 
@@ -342,7 +330,7 @@
         for h in range(heads):
             vk_total[h] = runs[h]
 
-        @pl.when(shard == 0)
+        @pl.when(jnp.logical_and(shard == 0, shard + 1 < shards))
         def _():
             pass_on(vk_total, vk_staged, vk_before, vk_send, vk_recv)
 
@@ -386,7 +374,7 @@
     causal = jnp.where(twice, lane - GROUP, lane) <= sub
 
     def finish(step, carry):
-        source = lax.rem(me + pick([*order_out, 0], step), owners)
+        source = lax.rem(me + 1 + step, owners)
         jobs = [(h, i) for h in range(heads) for i in range(per_source)]
         solved = []
         for h, i in jobs:

time: 51.7 us -> 49.5 us (0.957)
  Pallas kernels: 49.6 us -> 47.2 us
    pallas_call x1, Pallas kernels: 49.6 us -> 47.2 us  [body(): pl.pallas_call(functools.partial(whole_kernel, owners, shards), out_shape...]
where the time goes in v4:
time: 49.5 us; the launch traced here: 49.1 us
  Pallas kernels  47.2 us (95%)
  local copies, waits for them, and re-layouts  1.88 us (4%)
    pallas_call x1, Pallas kernels, body(): pl.pallas_call(functools.partial(whole_kernel, owners, shards), out_shape...  47.2 us
    unnamed x1, local copies, waits for them, and re-layouts  1.88 us

profile of v4, /device:TPU:27, one launch (start us, length us, event | category | flops | bytes accessed | tf_op | source)
XLA Modules:
  0.0 49.1 jit_solution(7637339102835829510)
XLA Ops:
  0.0 47.2 %shard_map.46 = bf16[128,2048]{1,0:T(8,128)(2,1)} custom-call(bf16[128,2048]{1,0:T(8,128)(2,1)} %q_hbm.1, bf16[128,2048]{1,0:T(8,128)(2,1)} %k_hbm.1, bf16[128,2048]{1,0:T(8,128)(2,1)} %v_hbm.1, f32[16,128]{1,0:T(8,128)} %ridge_ref.1), custom_call_target="tpu_custom_call" | custom-call | tf_op jit(solution)/shard_map/pallas_call | solution.py:439
  47.2 1.9 %copy.6 = bf16[128,2048]{1,0:T(8,128)(2,1)} copy(bf16[128,2048]{1,0:T(8,128)(2,1)} %shard_map.46) | data formatting | bytes 1048576
